TPU v7x, 32 devices: a whole 2x2x4 slice. The times are simulated.
32 devices in a mesh: dp: 4 (over z), mp: 8 (over y, x, core).
Axes of the slice: x: 2, y: 2, z: 4, core: 2. Of those that a mesh axis runs over, the one named last changes fastest.
Arguments:
- gradients: bfloat16 [4, 2, 768, 2048], P('dp', None, None, 'mp'), may hold values from -4 to 4
- weights: bfloat16 [2, 768, 2048], P(None, None, 'mp'), may hold values from -4 to 4
- projection: float32 [2, 768, 256], replicated, may hold values from -0.21875 to 0.21875
- moment_first: float32 [2, 256, 2048], P(None, 'dp', 'mp'), may hold values from -6 to 6
- moment_second: float32 [2, 256, 2048], P(None, 'dp', 'mp'), may hold values from 0.25 to 4
Outputs:
- new_weights: bfloat16 [2, 768, 2048], P(None, None, 'mp')
- new_first: float32 [2, 256, 2048], P(None, 'dp', 'mp')
- new_second: float32 [2, 256, 2048], P(None, 'dp', 'mp')
- new_bases: float32 [2, 768, 256], replicated
All inputs are finite; a program needn't handle non-finite values.
Results may differ from a plain program's by a relative error of at most 0.0004.
Values may be sent and summed in bfloat16 or wider, within the bound.
A program may use at most 64 MiB of HBM per device.

v0:
```python
import jax
import jax.numpy as jnp
from jax import lax
from jax.sharding import PartitionSpec as P

NS_ITERS = 4
beta_first = 0.5
beta_second = 0.5
adam_eps = 1e-06
learn_rate = 0.1


def newton_schulz(subspace):
    highest = lax.Precision.HIGHEST
    factor = 1.0 / (jnp.sqrt(jnp.sum(subspace * subspace, axis=(1, 2), keepdims=True)) + 1e-06)
    current = subspace * factor
    for sweep in range(NS_ITERS):
        gram = jnp.einsum("ldr,lds->lrs", current, current, precision=highest)
        current = 1.5 * current - 0.5 * jnp.einsum("ldr,lrs->lds", current, gram, precision=highest)
    return current


def back_project(bases_rows, direction_own):
    highest = lax.Precision.HIGHEST
    return jnp.einsum(
        "ldr,lrf->ldf",
        bases_rows,
        lax.all_gather(direction_own, "dp", axis=1, tiled=True),
        precision=highest,
    )


def shards(gradients, weights, projection, moment_first, moment_second):
    highest = lax.Precision.HIGHEST
    local_grad = gradients[0].astype(jnp.float32)
    totals = lax.psum(local_grad, "dp")
    lowrank = jnp.einsum("ldr,ldf->lrf", projection, totals, precision=highest)
    partial_sub = jnp.einsum("ldf,lrf->ldr", totals, lowrank, precision=highest)
    subspace = lax.psum(partial_sub, "mp")
    rank_rows = moment_first.shape[1]
    rank_start = lax.axis_index("dp") * rank_rows
    low_own = lax.dynamic_slice_in_dim(lowrank, rank_start, rank_rows, 1)
    new_first = beta_first * moment_first + (1.0 - beta_first) * low_own
    new_second = beta_second * moment_second + (1.0 - beta_second) * low_own * low_own
    direction_own = new_first / (jnp.sqrt(new_second) + adam_eps)
    width_rows = weights.shape[1] // lax.axis_size("dp")
    row_start = lax.axis_index("dp") * width_rows
    bases_rows = lax.dynamic_slice_in_dim(projection, row_start, width_rows, 1)
    weight_rows = lax.dynamic_slice_in_dim(weights, row_start, width_rows, 1)
    delta_rows = back_project(bases_rows, direction_own)
    updated = (weight_rows.astype(jnp.float32) - learn_rate * delta_rows).astype(jnp.bfloat16)
    new_weights = lax.all_gather(updated, "dp", axis=1, tiled=True)
    new_bases = newton_schulz(subspace)
    return (new_weights, new_first, new_second, new_bases)


def solution(mesh):
    placed = (
        P("dp", None, None, "mp"),
        P(None, None, "mp"),
        P(),
        P(None, "dp", "mp"),
        P(None, "dp", "mp"),
    )
    return jax.shard_map(
        shards,
        mesh=mesh,
        in_specs=placed,
        out_specs=(P(None, None, "mp"), P(None, "dp", "mp"), P(None, "dp", "mp"), P()),
        check_vma=False,
    )
```

profile of v0, /device:TPU:0, one launch (start us, length us, event | category | flops | bytes accessed | tf_op | source)
XLA Modules:
  0.0 174.0 jit_solution(6145538785186923639)
XLA Ops:
  7.2 2.5 %bitcast_convert_fusion = f32[2,768,256]{2,1,0:T(8,128)} fusion(bf16[1,2,768,256]{3,2,1,0:T(8,128)(2,1)} %param.5), kind=kLoop, calls=%fused_computation.12 | loop fusion | flops 393216 | bytes 2359296 | tf_op jit(solution)/shard_map/convert_element_type | solution.py:35
  9.8 0.0 all-reduce.5.cloned.1.call-start
  9.8 72.8 %all-reduce.3.cloned.1.call-done = f32[2,768,256]{2,1,0:T(8,128)} async-done(((f32[2,768,256]{2,1,0:T(8,128)}), f32[2,768,256]{2,1,0:T(8,128)}) %all-reduce.3.cloned.1.call-update) | async-done | bytes 1572880 | tf_op jit(solution)/shard_map/psum | solution.py:36
  82.7 4.2 %fusion.11 = f32[2,256,256]{2,1,0:T(8,128)S(1)} fusion(f32[2,768,256]{2,1,0:T(8,128)S(1)} %copy-done, f32[2,768,256]{2,1,0:T(8,128)} %all-reduce.3.cloned.1.call-done), kind=kOutput, calls=%fused_computation.22 | convolution fusion | flops 1207959552 | bytes 3670016 | tf_op jit(solution)/shard_map/ldr,ldf->lrf/dot_general | solution.py:37
  86.9 2.6 %convolution_bitcast_fusion = f32[2,768,256]{1,2,0:T(8,128)} fusion(f32[2,256,256]{2,1,0:T(8,128)S(1)} %fusion.11, f32[2,768,256]{2,1,0:T(8,128)S(1)} %copy-done.2), kind=kOutput, calls=%fused_computation.5 | convolution fusion | flops 1207959552 | bytes 3670016 | tf_op jit(solution)/shard_map/ldf,lrf->ldr/dot_general | solution.py:38
  89.5 0.9 copy-done.3
  90.4 0.1 copy-done.4
  90.5 0.8 add_divide_fusion
  91.2 15.7 %all_gather.6 = f32[2,256,256]{2,1,0:T(8,128)S(1)} all-gather(f32[2,64,256]{2,1,0:T(8,128)S(1)} %get-tuple-element.8), channel_id=1, replica_groups=mesh['dp'=4,'mp'=8] {'dp'}, dimensions={1}, use_global_device_ids=true | all-gather | bytes 655360 | tf_op jit(solution)/shard_map/all_gather | solution.py:28
  106.9 1.5 fusion.4
  108.4 18.3 %all_gather.7 = bf16[2,768,256]{2,1,0:T(8,128)(2,1)} all-gather(bf16[2,192,256]{2,1,0:T(8,128)(2,1)S(1)} %fusion.4), channel_id=1, replica_groups=mesh['dp'=4,'mp'=8] {'dp'}, dimensions={1}, use_global_device_ids=true | all-gather | bytes 983040 | tf_op jit(solution)/shard_map/all_gather | solution.py:52
  126.7 20.9 %all-reduce.5.cloned.1.call-done = f32[2,768,256]{1,2,0:T(8,128)} async-done(((f32[2,768,256]{1,2,0:T(8,128)}), f32[2,768,256]{1,2,0:T(8,128)}) %all-reduce.5.cloned.1.call-update) | async-done | bytes 1572880 | tf_op jit(solution)/shard_map/psum | solution.py:39
  147.6 1.8 %multiply_reduce_fusion = f32[2]{0:T(128)S(1)} fusion(f32[2,768,256]{1,2,0:T(8,128)} %all-reduce.5.cloned.1.call-done), kind=kLoop, calls=%fused_computation.4 | loop fusion | flops 786430 | bytes 1572872 | tf_op jit(solution)/shard_map/reduce_sum | solution.py:15
  149.4 0.0 copy-done.1
  149.5 1.8 %fusion = f32[2,256,256]{2,1,0:T(8,128)S(1)} fusion(f32[2,768,256]{1,2,0:T(8,128)S(1)} %copy-done.1, f32[2]{0:T(128)S(1)} %add_divide_fusion.1), kind=kOutput, calls=%fused_computation.6 | convolution fusion | flops 1208352768 | bytes 2097160 | tf_op jit(solution)/shard_map/ldr,lds->lrs/dot_general | solution.py:18
  151.2 2.0 %multiply_subtract_fusion.3 = f32[2,768,256]{1,2,0:T(8,128)S(1)} fusion(f32[2,256,256]{2,1,0:T(8,128)S(1)} %fusion, f32[2,768,256]{1,2,0:T(8,128)S(1)} %copy-done.1, f32[2]{0:T(128)S(1)} %add_divide_fusion.1), kind=kOutput, calls=%fused_computation.3 | convolution fusion | flops 1209925632 | bytes 3670024 | tf_op jit(solution)/shard_map/ldr,lrs->lds/dot_general | solution.py:19
  153.2 1.6 fusion.12
  154.9 1.8 %multiply_subtract_fusion.2 = f32[2,768,256]{1,2,0:T(8,128)S(1)} fusion(f32[2,768,256]{1,2,0:T(8,128)S(1)} %multiply_subtract_fusion.3, f32[2,256,256]{2,1,0:T(8,128)S(1)} %fusion.12), kind=kOutput, calls=%fused_computation.2 | convolution fusion | flops 1209139200 | bytes 3670016 | tf_op jit(solution)/shard_map/ldr,lrs->lds/dot_general | solution.py:19
  156.6 1.6 fusion.13
  158.3 1.8 %multiply_subtract_fusion.1 = f32[2,768,256]{1,2,0:T(8,128)S(1)} fusion(f32[2,768,256]{1,2,0:T(8,128)S(1)} %multiply_subtract_fusion.2, f32[2,256,256]{2,1,0:T(8,128)S(1)} %fusion.13), kind=kOutput, calls=%fused_computation.1 | convolution fusion | flops 1209139200 | bytes 3670016 | tf_op jit(solution)/shard_map/ldr,lrs->lds/dot_general | solution.py:19
  160.1 1.6 fusion.14
  161.7 1.8 %multiply_subtract_fusion = f32[2,768,256]{1,2,0:T(8,128)S(1)} fusion(f32[2,768,256]{1,2,0:T(8,128)S(1)} %multiply_subtract_fusion.1, f32[2,256,256]{2,1,0:T(8,128)S(1)} %fusion.14), kind=kOutput, calls=%fused_computation | convolution fusion | flops 1209139200 | bytes 3670016 | tf_op jit(solution)/shard_map/ldr,lrs->lds/dot_general | solution.py:19
  163.5 1.6 copy.18
  165.1 2.1 %copy.31 = bf16[2,768,256]{2,1,0:T(8,128)(2,1)} copy(bf16[2,768,256]{2,1,0:T(8,128)(2,1)} %all_gather.7) | data formatting | bytes 1572864
  (11 shorter events, 0.1 us)
Async XLA Ops:
  7.2 75.5 %copy-start = (f32[2,768,256]{2,1,0:T(8,128)S(1)}, f32[2,768,256]{2,1,0:T(8,128)}, u32[]{:S(2)}) copy-start(f32[2,768,256]{2,1,0:T(8,128)} %param.7) | copy-start | bytes 4718596
  7.2 75.5 %all-reduce.3.cloned.1.call-start = ((), (), s32[]{:S(2)}) async-start(), calls=%async_computation | async-start | bytes 3145728 | tf_op jit(solution)/shard_map/psum | solution.py:36
  9.8 137.8 %all-reduce.5.cloned.1.call-start = ((), (), s32[]{:S(2)}) async-start(), calls=%async_computation.1 | async-start | bytes 3145728 | tf_op jit(solution)/shard_map/psum | solution.py:39
  82.7 4.2 %copy-start.2 = (f32[2,768,256]{2,1,0:T(8,128)S(1)}, f32[2,768,256]{2,1,0:T(8,128)}, u32[]{:S(2)}) copy-start(f32[2,768,256]{2,1,0:T(8,128)} %all-reduce.3.cloned.1.call-done) | copy-start | bytes 4718596
  89.5 0.9 copy-start.3
  89.5 1.0 copy-start.4
  147.6 1.9 %copy-start.1 = (f32[2,768,256]{1,2,0:T(8,128)S(1)}, f32[2,768,256]{1,2,0:T(8,128)}, u32[]{:S(2)}) copy-start(f32[2,768,256]{1,2,0:T(8,128)} %all-reduce.5.cloned.1.call-done) | copy-start | bytes 4718596
Sparse Core Ops, SparseCore 0:
  10.9 71.6 all-reduce.2
  89.7 57.8 all-reduce.4
where the time goes:
time: 174 us
  waiting for transfers between devices  93.7 us (54%)
  blocking collectives  34 us (20%)
  matrix products  22.3 us (13%)
  between operations  14.1 us (8%)
  other arithmetic  5.1 us (3%)
  local copies, waits for them, and re-layouts  4.67 us (3%)
    psum x1, waiting for transfers between devices, shards(): totals = lax.psum(local_grad, 'dp')  72.8 us
    psum x1, waiting for transfers between devices, shards(): subspace = lax.psum(partial_sub, 'mp')  20.9 us
    all_gather x1, blocking collectives, shards(): new_weights = lax.all_gather(updated, 'dp', axis=1, tiled=True)  18.3 us
    all_gather x1, blocking collectives, back_project(): lax.all_gather(direction_own, 'dp', axis=1, tiled=True)  15.7 us
    dot_general x4, matrix products, newton_schulz(): jnp.einsum('ldr,lrs->lds', current, gram, precision=highest)  7.29 us
    dot_general x4, matrix products, newton_schulz(): gram = jnp.einsum('ldr,lds->lrs', current, current, precision=highest)  6.66 us
    unnamed x12, local copies, waits for them, and re-layouts  4.67 us
    dot_general x1, matrix products, shards(): lowrank = jnp.einsum('ldr,ldf->lrf', projection, totals, precision=highest)  4.21 us
  transfers between devices with their start and end apart: 2, of which 2 were waited for; matrix products, arithmetic and copies ran while one was open for 1% of the time, Pallas kernels for 0%

commit v1 on v0

--- a/solution.py
+++ b/solution.py
@@ -33,7 +33,9 @@
 def shards(gradients, weights, projection, moment_first, moment_second):
     highest = lax.Precision.HIGHEST
     local_grad = gradients[0].astype(jnp.float32)
-    totals = lax.psum(local_grad, "dp")
+    totals = local_grad
+    for hop in (1, 2):
+        totals = totals + lax.ppermute(totals, "dp", [(dev, dev ^ hop) for dev in range(4)])
     lowrank = jnp.einsum("ldr,ldf->lrf", projection, totals, precision=highest)
     partial_sub = jnp.einsum("ldf,lrf->ldr", totals, lowrank, precision=highest)
     subspace = lax.psum(partial_sub, "mp")

time: 174 us -> 213 us (1.22)
  waiting for transfers between devices: 93.7 us -> 124 us
  starting transfers between devices: 0.08 us -> 5.97 us
  matrix products: 22.3 us -> 26.3 us
  local copies, waits for them, and re-layouts: 4.67 us -> 1.88 us
    ppermute x0 -> x2, waiting for transfers between devices: none -> 102 us  [shards(): lax.ppermute(totals, 'dp', [(dev, dev ^ hop) for dev in range(4)])]
    psum x1 -> x0, waiting for transfers between devices: 72.8 us -> none  [shards(): totals = lax.psum(local_grad, 'dp')]
    ppermute x0 -> x2, starting transfers between devices: none -> 5.94 us  [shards(): lax.ppermute(totals, 'dp', [(dev, dev ^ hop) for dev in range(4)])]
    dot_general x4, matrix products: 6.66 us -> 11.3 us  [newton_schulz(): gram = jnp.einsum('ldr,lds->lrs', current, current, precision=highest)]
    unnamed x12 -> x11, local copies, waits for them, and re-layouts: 4.67 us -> 1.88 us
  transfers between devices with their start and end apart: 2 -> 3, of which waited for: 2 -> 3; matrix products, arithmetic and copies ran while one was open for 1% -> 1% of each run, Pallas kernels for 0% -> 0%
where the time goes in v1:
time: 213 us
  waiting for transfers between devices  124 us (58%)
  blocking collectives  34.4 us (16%)
  matrix products  26.3 us (12%)
  between operations  14.1 us (7%)
  starting transfers between devices  5.97 us (3%)
  other arithmetic  5.76 us (3%)
    ppermute x2, waiting for transfers between devices, shards(): lax.ppermute(totals, 'dp', [(dev, dev ^ hop) for dev in range(4)])  102 us
    psum x1, waiting for transfers between devices, shards(): subspace = lax.psum(partial_sub, 'mp')  22.2 us
    all_gather x1, blocking collectives, shards(): new_weights = lax.all_gather(updated, 'dp', axis=1, tiled=True)  18.7 us
    all_gather x1, blocking collectives, back_project(): lax.all_gather(direction_own, 'dp', axis=1, tiled=True)  15.7 us
    dot_general x4, matrix products, newton_schulz(): gram = jnp.einsum('ldr,lds->lrs', current, current, precision=highest)  11.3 us
    dot_general x4, matrix products, newton_schulz(): jnp.einsum('ldr,lrs->lds', current, gram, precision=highest)  8.14 us
    ppermute x2, starting transfers between devices, shards(): lax.ppermute(totals, 'dp', [(dev, dev ^ hop) for dev in range(4)])  5.94 us
  transfers between devices with their start and end apart: 3, of which 3 were waited for; matrix products, arithmetic and copies ran while one was open for 1% of the time, Pallas kernels for 0%

profile of v1, /device:TPU:0, one launch (start us, length us, event | category | flops | bytes accessed | tf_op | source)
XLA Modules:
  0.0 212.6 jit_solution(7418779889391960890)
XLA Ops:
  7.2 1.4 bitcast_convert_fusion
  8.6 3.1 %collective-permute-start = (f32[2,768,256]{2,1,0:T(8,128)S(1)}, f32[2,768,256]{2,1,0:T(8,128)S(1)}, u32[]{:S(2)}, u32[]{:S(2)}) collective-permute-start(f32[2,768,256]{2,1,0:T(8,128)S(1)} %bitcast_convert_fusion), channel_id=1, source_target_pairs={{0,8},{8,0},{16,24},{24,16},{1,9},{9,1},{17,25},{25,17},{2,10},{10... | collective-permute-start | bytes 4718600 | tf_op jit(solution)/shard_map/ppermute | solution.py:38
  11.8 34.4 %collective-permute-done = f32[2,768,256]{2,1,0:T(8,128)S(1)} collective-permute-done((f32[2,768,256]{2,1,0:T(8,128)S(1)}, f32[2,768,256]{2,1,0:T(8,128)S(1)}, u32[]{:S(2)}, u32[]{:S(2)}) %collective-permute-start) | collective-permute-done | bytes 1572896 | tf_op jit(solution)/shard_map/ppermute | solution.py:38
  46.3 2.8 %collective-permute-start.1 = (f32[2,768,256]{2,1,0:T(8,128)S(1)}, f32[2,768,256]{2,1,0:T(8,128)}, u32[]{:S(2)}, u32[]{:S(2)}) collective-permute-start(f32[2,768,256]{2,1,0:T(8,128)S(1)} %fusion.7), channel_id=1, source_target_pairs={{0,16},{8,24},{16,0},{24,8},{1,17},{9,25},{17,1},{25,9},{2,18},{10... | collective-permute-start | bytes 4718600 | tf_op jit(solution)/shard_map/ppermute | solution.py:38
  49.1 67.5 %collective-permute-done.1 = f32[2,768,256]{2,1,0:T(8,128)} collective-permute-done((f32[2,768,256]{2,1,0:T(8,128)S(1)}, f32[2,768,256]{2,1,0:T(8,128)}, u32[]{:S(2)}, u32[]{:S(2)}) %collective-permute-start.1) | collective-permute-done | bytes 1572896 | tf_op jit(solution)/shard_map/ppermute | solution.py:38
  116.7 1.6 add.37
  118.3 2.7 %fusion.12 = f32[2,256,256]{1,2,0:T(8,128)S(1)} fusion(f32[2,768,256]{2,1,0:T(8,128)S(1)} %add.37, f32[2,768,256]{2,1,0:T(8,128)S(1)} %copy-done), kind=kOutput, calls=%fused_computation.22 | convolution fusion | flops 1207959552 | bytes 3670016 | tf_op jit(solution)/shard_map/ldr,ldf->lrf/dot_general | solution.py:39
  121.0 2.7 %fusion.13 = f32[2,768,256]{2,1,0:T(8,128)} fusion(f32[2,768,256]{2,1,0:T(8,128)S(1)} %add.37, f32[2,256,256]{1,2,0:T(8,128)S(1)} %fusion.12), kind=kOutput, calls=%fused_computation.23 | convolution fusion | flops 1207959552 | bytes 3670016 | tf_op jit(solution)/shard_map/ldf,lrf->ldr/dot_general | solution.py:40
  123.7 0.9 copy-done.3
  124.6 0.8 add_divide_fusion
  125.4 15.7 %all_gather.6 = f32[2,256,256]{2,1,0:T(8,128)S(1)} all-gather(f32[2,64,256]{2,1,0:T(8,128)S(1)} %get-tuple-element.4), channel_id=1, replica_groups=mesh['dp'=4,'mp'=8] {'dp'}, dimensions={1}, use_global_device_ids=true | all-gather | bytes 655360 | tf_op jit(solution)/shard_map/all_gather | solution.py:28
  141.1 1.5 fusion.4
  142.6 18.7 %all_gather.7 = bf16[2,768,256]{2,1,0:T(8,128)(2,1)S(1)} all-gather(bf16[2,192,256]{2,1,0:T(8,128)(2,1)S(1)} %fusion.4), channel_id=1, replica_groups=mesh['dp'=4,'mp'=8] {'dp'}, dimensions={1}, use_global_device_ids=true | all-gather | bytes 983040 | tf_op jit(solution)/shard_map/all_gather | solution.py:54
  161.3 22.2 %all-reduce.2.cloned.1.call-done = f32[2,768,256]{2,1,0:T(8,128)} async-done(((f32[2,768,256]{2,1,0:T(8,128)}), f32[2,768,256]{2,1,0:T(8,128)}) %all-reduce.2.cloned.1.call-update) | async-done | bytes 1572880 | tf_op jit(solution)/shard_map/psum | solution.py:41
  183.6 1.8 multiply_reduce_fusion
  185.4 2.8 %fusion = f32[2,256,256]{2,1,0:T(8,128)S(1)} fusion(f32[2,768,256]{2,1,0:T(8,128)S(1)} %copy-done.1, f32[2]{0:T(128)S(1)} %add_divide_fusion.1), kind=kOutput, calls=%fused_computation.5 | convolution fusion | flops 1208352768 | bytes 2097160 | tf_op jit(solution)/shard_map/ldr,lds->lrs/dot_general | solution.py:18
  188.3 1.7 multiply_subtract_fusion.3
  190.0 2.8 %fusion.14 = f32[2,256,256]{2,1,0:T(8,128)S(1)} fusion(f32[2,768,256]{2,1,0:T(8,128)S(1)} %multiply_subtract_fusion.3), kind=kOutput, calls=%fused_computation.24 | convolution fusion | flops 1207959552 | bytes 2097152 | tf_op jit(solution)/shard_map/ldr,lds->lrs/dot_general | solution.py:18
  192.9 1.7 multiply_subtract_fusion.2
  194.6 2.8 %fusion.15 = f32[2,256,256]{2,1,0:T(8,128)S(1)} fusion(f32[2,768,256]{2,1,0:T(8,128)S(1)} %multiply_subtract_fusion.2), kind=kOutput, calls=%fused_computation.25 | convolution fusion | flops 1207959552 | bytes 2097152 | tf_op jit(solution)/shard_map/ldr,lds->lrs/dot_general | solution.py:18
  197.4 1.9 multiply_subtract_fusion.1
  199.3 2.8 %fusion.16 = f32[2,256,256]{2,1,0:T(8,128)S(1)} fusion(f32[2,768,256]{2,1,0:T(8,128)S(1)} %multiply_subtract_fusion.1), kind=kOutput, calls=%fused_computation.26 | convolution fusion | flops 1207959552 | bytes 2097152 | tf_op jit(solution)/shard_map/ldr,lds->lrs/dot_general | solution.py:18
  202.1 2.8 %multiply_subtract_fusion = f32[2,768,256]{2,1,0:T(8,128)} fusion(f32[2,768,256]{2,1,0:T(8,128)S(1)} %multiply_subtract_fusion.1, f32[2,256,256]{2,1,0:T(8,128)S(1)} %fusion.16), kind=kOutput, calls=%fused_computation | convolution fusion | flops 1209139200 | bytes 3670016 | tf_op jit(solution)/shard_map/ldr,lrs->lds/dot_general | solution.py:19
  204.9 0.9 copy.15
  (13 shorter events, 0.3 us)
Async XLA Ops:
  7.2 111.1 %copy-start = (f32[2,768,256]{2,1,0:T(8,128)S(1)}, f32[2,768,256]{2,1,0:T(8,128)}, u32[]{:S(2)}) copy-start(f32[2,768,256]{2,1,0:T(8,128)} %param.7) | copy-start | bytes 4718596
  7.2 176.4 %all-reduce.2.cloned.1.call-start = ((), (), s32[]{:S(2)}) async-start(), calls=%async_computation | async-start | bytes 3145728 | tf_op jit(solution)/shard_map/psum | solution.py:41
  7.2 38.9 %copy-start.2 = (bf16[1,2,768,256]{3,2,1,0:T(8,128)(2,1)S(1)}, bf16[1,2,768,256]{3,2,1,0:T(8,128)(2,1)}, u32[]{:S(2)}) copy-start(bf16[1,2,768,256]{3,2,1,0:T(8,128)(2,1)} %param.5) | copy-start | bytes 2359300
  8.6 37.5 %collective-permute-start = (f32[2,768,256]{2,1,0:T(8,128)S(1)}, f32[2,768,256]{2,1,0:T(8,128)S(1)}, u32[]{:S(2)}, u32[]{:S(2)}) collective-permute-start(f32[2,768,256]{2,1,0:T(8,128)S(1)} %bitcast_convert_fusion), channel_id=1, source_target_pairs={{0,8},{8,0},{16,24},{24,16},{1,9},{9,1},{17,25},{25,17},{2,10},{10... | collective-permute-start | bytes 4718600 | tf_op jit(solution)/shard_map/ppermute | solution.py:38
  46.3 70.3 %collective-permute-start.1 = (f32[2,768,256]{2,1,0:T(8,128)S(1)}, f32[2,768,256]{2,1,0:T(8,128)}, u32[]{:S(2)}, u32[]{:S(2)}) collective-permute-start(f32[2,768,256]{2,1,0:T(8,128)S(1)} %fusion.7), channel_id=1, source_target_pairs={{0,16},{8,24},{16,0},{24,8},{1,17},{9,25},{17,1},{25,9},{2,18},{10... | collective-permute-start | bytes 4718600 | tf_op jit(solution)/shard_map/ppermute | solution.py:38
  123.6 0.9 copy-start.3
  123.7 1.0 copy-start.4
  183.6 1.9 copy-start.1
Sparse Core Ops, SparseCore 0:
  123.8 59.7 all-reduce.1
